TPU v7x, 512 devices: a whole 4x4x16 slice. The times are simulated.
512 devices in a mesh: mpo: 16 (over y, x), sector: 32 (over z, core).
Axes of the slice: x: 4, y: 4, z: 16, core: 2. Of those that a mesh axis runs over, the one named last changes fastest.
Arguments:
- wavefunction: bfloat16 [128, 512, 512], P('sector'), may hold values from -6 to 6
- left_env: bfloat16 [16, 128, 512, 512], P('mpo', 'sector'), may hold values from -0.375 to 0.375
- right_env: bfloat16 [16, 128, 512, 512], P('mpo', 'sector'), may hold values from -0.0625 to 0.0625
- mpo_mask: int32 [16, 128], P('mpo', 'sector'), may hold values 0 or 1
- block_size: int32 [128], P('sector'), may hold values from 64 to 512, as said below
- route_owner: int32 [16, 128, 8], P('mpo', 'sector'), may hold values from 0 to 31, all different within a row; in each aligned block of 4 rows (0 to 3, 4 to 7, ..., all dimensions but the last counted through in order) at most 2 rows name the same one
- route_block: int32 [16, 128, 8], P('mpo', 'sector'), may hold values from 0 to 3
Outputs:
- sigma_right: bfloat16 [128, 512, 512], P('sector', 'mpo')
Inputs may be any that keep to these rules, and one draw needn't show every extreme that they name: `block_size`: some block in every draw has all 512 states live. `route_owner`: each row (m, b) names 8 different owners. Among the 4 rows of one device (one m and the blocks of one sector owner) no owner is named more than 2 times, and in some device's rows some owner is named exactly 2 times; every owner is named somewhere.
All inputs are finite; a program needn't handle non-finite values. No bound on the sum of `mpo_mask` on one device may be relied on, other than what follows from the above.
Results may differ from a plain program's by a relative error of at most 0.014.
Values may be sent and summed in bfloat16 or wider, within the bound.
A program may use at most 64 MiB of HBM per device.

v0:
```python
import jax
import jax.numpy as jnp
from jax import lax
from jax.sharding import PartitionSpec as P

ROW_GROUPS = 4
COL_PARTS = 2
PIECES = 8


def cut_along(x, dim, devices):
    before, after = (x.shape[:dim], x.shape[dim + 1 :])
    return jnp.moveaxis(x.reshape(*before, devices, -1, *after), dim, 0)


def sent_and_summed(x, axis, dim):
    tiles = cut_along(x, dim, lax.axis_size(axis))
    arrived = lax.all_to_all(tiles, axis, split_axis=0, concat_axis=0, tiled=True)
    return arrived.astype(jnp.float32).sum(axis=0)


def per_device(wavefunction, left_env, right_env, mpo_mask, block_size, route_owner, route_block):
    block_count = wavefunction.shape[0]
    states = wavefunction.shape[1]
    row_count = states // lax.axis_size("mpo")
    positions = jnp.arange(states, dtype=jnp.int32)
    live_cols = positions[None, :] < block_size[:, None]
    live_mask = live_cols[:, :, None] & live_cols[:, None, :]
    masked = jnp.where(live_mask, wavefunction, jnp.zeros_like(wavefunction))
    right_part = jnp.einsum(
        "bij,bkj->bik", masked, right_env[0], preferred_element_type=jnp.float32
    ).astype(jnp.bfloat16)
    factor = mpo_mask[0].astype(jnp.float32)
    left_rows = left_env[0]
    product = jnp.einsum("bij,bjk->ibk", left_rows, right_part, preferred_element_type=jnp.float32)
    row_share = sent_and_summed((product * factor[None, :, None]).astype(jnp.bfloat16), "mpo", 0)
    global_rows = lax.axis_index("mpo") * row_count + jnp.arange(row_count, dtype=jnp.int32)
    live_rows = global_rows[:, None] < block_size[None, :]
    share_mask = live_rows[:, :, None] & live_cols[None, :, :]
    sigma_share = jnp.where(share_mask, row_share, jnp.zeros_like(row_share)).astype(jnp.bfloat16)
    group_rows = row_count // ROW_GROUPS
    width_part = states // COL_PARTS
    pieces = sigma_share.reshape(ROW_GROUPS, group_rows, block_count, COL_PARTS, width_part)
    pieces = pieces.transpose(2, 0, 3, 1, 4).reshape(block_count * PIECES, group_rows * width_part)
    owners = route_owner[0].reshape(-1)
    target_code = (route_block[0] * PIECES + jnp.arange(PIECES, dtype=jnp.int32)[None, :]).reshape(
        -1
    )
    peer_count = lax.axis_size("sector")
    capacity = min(block_count, max(2, (2 * block_count * PIECES + peer_count - 1) // peer_count))
    is_owner = (owners[:, None] == jnp.arange(peer_count, dtype=jnp.int32)[None, :]).astype(
        jnp.int32
    )
    before = jnp.cumsum(is_owner, axis=0) - is_owner
    position = jnp.sum(before * is_owner, axis=1)
    destination = owners * capacity + position
    slot_ids = jnp.arange(peer_count * capacity, dtype=jnp.int32)
    placing = slot_ids[:, None] == destination[None, :]
    send_data = jnp.dot(
        placing.astype(jnp.bfloat16), pieces, preferred_element_type=jnp.float32
    ).astype(jnp.bfloat16)
    send_data = send_data.reshape(peer_count, capacity, group_rows * width_part)
    send_code = (
        jnp.sum(placing.astype(jnp.int32) * (target_code + 1)[None, :], axis=1) - 1
    ).reshape(peer_count, capacity)
    arrived_data, arrived_code = (
        lax.all_to_all(send_data, "sector", split_axis=0, concat_axis=0, tiled=True),
        lax.all_to_all(send_code, "sector", split_axis=0, concat_axis=0, tiled=True),
    )
    arrived_data = arrived_data.reshape(peer_count * capacity, group_rows * width_part)
    arrived_code = arrived_code.reshape(-1)
    targets = jnp.arange(block_count * PIECES, dtype=jnp.int32)
    collect = (arrived_code[None, :] == targets[:, None]).astype(jnp.bfloat16)
    landed = jnp.dot(collect, arrived_data, preferred_element_type=jnp.float32).astype(jnp.bfloat16)
    landed = landed.reshape(block_count, ROW_GROUPS, COL_PARTS, group_rows, width_part)
    return landed.transpose(0, 1, 3, 2, 4).reshape(block_count, row_count, states)


def solution(mesh):
    placed = (
        P("sector", None, None),
        P("mpo", "sector", None, None),
        P("mpo", "sector", None, None),
        P("mpo", "sector"),
        P("sector"),
        P("mpo", "sector", None),
        P("mpo", "sector", None),
    )
    return jax.shard_map(
        per_device, mesh=mesh, in_specs=placed, out_specs=P("sector", "mpo", None), check_vma=False
    )
```

profile of v0, /device:TPU:1, one launch (start us, length us, event | category | flops | bytes accessed | tf_op | source)
XLA Modules:
  0.0 105.3 jit_solution(12229262630169752243)
XLA Ops:
  0.0 0.0 copy-start
  0.0 0.8 convert_bitcast_fusion
  0.8 0.7 iota_compare_fusion.5
  1.5 0.1 copy-done
  1.6 5.9 %multiply_convert_fusion = bf16[4,512,512]{1,2,0:T(8,128)(2,1)} fusion(bf16[1,4,512,512]{3,2,1,0:T(8,128)(2,1)S(1)} %copy-done, f32[4]{0:T(128)S(1)} %convert_bitcast_fusion, bf16[4,512,512]{2,1,0:T(8,128)(2,1)} %param.7, bf16[1,4,512,512]{3,2,1,0:T(8,128)(2,1)} %param.9, pred[4,512]{1,0:T(4,128)(4,1)S(1)} %iota_compare_fusion.5), kind=kOutput, calls=%fused_computation.1 | convolution fusion | flops 2152726528 | bytes 8390672 | tf_op jit(solution)/shard_map/bij,bjk->ibk/dot_general | solution.py:35
  7.5 3.2 %copy.13 = bf16[16,32,4,512]{3,1,2,0:T(8,128)(2,1)} copy(bf16[16,32,4,512]{3,1,0,2:T(8,128)(2,1)} %bitcast.32) | data formatting | bytes 4194304 | tf_op jit(solution)/shard_map/reshape | solution.py:13
  10.7 0.0 copy-start.3
  10.7 0.0 copy-start.2
  10.7 0.0 copy-start.1
  10.7 7.8 %all-to-all-start.1 = ((bf16[16,32,4,512]{3,1,2,0:T(8,128)(2,1)}), bf16[16,32,4,512]{3,1,2,0:T(8,128)(2,1)}, u32[]{:S(2)}, u32[]{:S(2)}) async-start(bf16[16,32,4,512]{3,1,2,0:T(8,128)(2,1)} %copy.13), calls=%async_computation.1 | async-start | bytes 4194304 | tf_op jit(solution)/shard_map/all_to_all | solution.py:18
  18.5 0.0 copy-done.3
  18.5 0.1 mul.52
  18.6 0.1 add.57
  18.7 0.0 copy-done.2
  18.7 0.1 reshape_squeeze.3
  18.8 0.1 fusion.14
  18.8 0.1 reduce_window_sum.11
  18.9 0.2 select_reduce_fusion.1
  19.1 0.1 select_reduce_fusion
  19.2 0.7 sub.11
  19.9 0.0 copy-done.1
  19.9 0.1 broadcast_compare_fusion.1
  20.0 0.1 broadcast_compare_fusion
  20.1 23.2 %all-to-all-done.1 = bf16[16,32,4,512]{3,1,2,0:T(8,128)(2,1)} async-done(((bf16[16,32,4,512]{3,1,2,0:T(8,128)(2,1)}), bf16[16,32,4,512]{3,1,2,0:T(8,128)(2,1)}, u32[]{:S(2)}, u32[]{:S(2)}) %all-to-all-start.1) | async-done | bytes 2097184 | tf_op jit(solution)/shard_map/all_to_all | solution.py:18
  43.3 23.2 %all-to-all-start = ((s32[32,1,2]{2,1,0:T(1,128)}), s32[32,1,2]{2,1,0:T(1,128)S(1)}, u32[]{:S(2)}, u32[]{:S(2)}) async-start(s32[32,1,2]{2,1,0:T(1,128)} %bitcast), calls=%async_computation | async-start | bytes 32768 | tf_op jit(solution)/shard_map/all_to_all | solution.py:68
  66.5 1.9 %convert_reduce_fusion = bf16[32,4,512]{2,0,1:T(8,128)(2,1)S(1)} fusion(bf16[16,32,4,512]{3,1,2,0:T(8,128)(2,1)} %all-to-all-done.1), kind=kLoop, calls=%fused_computation | loop fusion | flops 2031616 | bytes 2228224 | tf_op jit(solution)/shard_map/reduce_sum | solution.py:19
  68.5 0.2 fusion.13
  68.8 0.3 convolution_convert_fusion
  69.1 0.9 reshape.160
  70.0 8.3 %all-to-all-done = s32[32,1,2]{2,1,0:T(1,128)S(1)} async-done(((s32[32,1,2]{2,1,0:T(1,128)}), s32[32,1,2]{2,1,0:T(1,128)S(1)}, u32[]{:S(2)}, u32[]{:S(2)}) %all-to-all-start) | async-done | bytes 288 | tf_op jit(solution)/shard_map/all_to_all | solution.py:68
  78.3 4.4 %all-to-all-start.2 = ((bf16[32,2,2048]{2,1,0:T(2,128)(2,1)}), bf16[32,2,2048]{2,1,0:T(2,128)(2,1)S(1)}, u32[]{:S(2)}, u32[]{:S(2)}) async-start(bf16[32,2,2048]{2,1,0:T(2,128)(2,1)} %reshape.160), calls=%async_computation.2 | async-start | bytes 524288 | tf_op jit(solution)/shard_map/all_to_all | solution.py:67
  82.7 0.5 broadcast.109
  83.2 0.7 reduce.3
  83.9 0.1 eq.47
  84.0 20.3 %all-to-all-done.2 = bf16[32,2,2048]{2,1,0:T(2,128)(2,1)S(1)} async-done(((bf16[32,2,2048]{2,1,0:T(2,128)(2,1)}), bf16[32,2,2048]{2,1,0:T(2,128)(2,1)S(1)}, u32[]{:S(2)}, u32[]{:S(2)}) %all-to-all-start.2) | async-done | bytes 262176 | tf_op jit(solution)/shard_map/all_to_all | solution.py:67
  104.3 0.1 reshape.161
  104.4 0.2 convolution_convert_fusion.1
  104.6 0.7 copy.16
  (9 shorter events, 0.1 us)
Async XLA Ops:
  0.0 1.6 %copy-start = (bf16[1,4,512,512]{3,2,1,0:T(8,128)(2,1)S(1)}, bf16[1,4,512,512]{3,2,1,0:T(8,128)(2,1)}, u32[]{:S(2)}) copy-start(bf16[1,4,512,512]{3,2,1,0:T(8,128)(2,1)} %param.8) | copy-start | bytes 6291460
  10.7 7.8 %copy-start.3 = (s32[1,4,8]{2,1,0:T(4,128)S(1)}, s32[1,4,8]{2,1,0:T(4,128)}, u32[]{:S(2)}) copy-start(s32[1,4,8]{2,1,0:T(4,128)} %param.13) | copy-start | bytes 388
  10.7 8.0 %copy-start.2 = (s32[1,4,8]{2,1,0:T(4,128)S(1)}, s32[1,4,8]{2,1,0:T(4,128)}, u32[]{:S(2)}) copy-start(s32[1,4,8]{2,1,0:T(4,128)} %param.12) | copy-start | bytes 388
  10.7 9.2 %copy-start.1 = (s32[4]{0:T(128)S(1)}, s32[4]{0:T(128)}, u32[]{:S(2)}) copy-start(s32[4]{0:T(128)} %param.11) | copy-start | bytes 52
  10.7 32.6 %all-to-all-start.1 = ((bf16[16,32,4,512]{3,1,2,0:T(8,128)(2,1)}), bf16[16,32,4,512]{3,1,2,0:T(8,128)(2,1)}, u32[]{:S(2)}, u32[]{:S(2)}) async-start(bf16[16,32,4,512]{3,1,2,0:T(8,128)(2,1)} %copy.13), calls=%async_computation.1 | async-start | bytes 4194304 | tf_op jit(solution)/shard_map/all_to_all | solution.py:18
  43.3 34.9 %all-to-all-start = ((s32[32,1,2]{2,1,0:T(1,128)}), s32[32,1,2]{2,1,0:T(1,128)S(1)}, u32[]{:S(2)}, u32[]{:S(2)}) async-start(s32[32,1,2]{2,1,0:T(1,128)} %bitcast), calls=%async_computation | async-start | bytes 32768 | tf_op jit(solution)/shard_map/all_to_all | solution.py:68
  78.3 26.1 %all-to-all-start.2 = ((bf16[32,2,2048]{2,1,0:T(2,128)(2,1)}), bf16[32,2,2048]{2,1,0:T(2,128)(2,1)S(1)}, u32[]{:S(2)}, u32[]{:S(2)}) async-start(bf16[32,2,2048]{2,1,0:T(2,128)(2,1)} %reshape.160), calls=%async_computation.2 | async-start | bytes 524288 | tf_op jit(solution)/shard_map/all_to_all | solution.py:67
where the time goes:
time: 106 us; the launch traced here: 105 us
  waiting for transfers between devices  51.8 us (49%)
  starting transfers between devices  35.4 us (33%)
  local copies, waits for them, and re-layouts  6.6 us (6%)
  matrix products  6.42 us (6%)
  other arithmetic  4.95 us (5%)
    all_to_all x1, waiting for transfers between devices, sent_and_summed(): lax.all_to_all(tiles, axis, split_axis=0, concat_axis=0, tiled=True)  23.2 us
    all_to_all x1, starting transfers between devices, per_device(): lax.all_to_all(send_code, 'sector', split_axis=0, concat_axis=0, tiled=True)  23.2 us
    all_to_all x1, waiting for transfers between devices, per_device(): lax.all_to_all(send_data, 'sector', split_axis=0, concat_axis=0, tiled=True)  20.3 us
    all_to_all x1, waiting for transfers between devices, per_device(): lax.all_to_all(send_code, 'sector', split_axis=0, concat_axis=0, tiled=True)  8.27 us
    all_to_all x1, starting transfers between devices, sent_and_summed(): lax.all_to_all(tiles, axis, split_axis=0, concat_axis=0, tiled=True)  7.76 us
    dot_general x1, matrix products, per_device(): jnp.einsum('bij,bjk->ibk', left_rows, right_part, preferred_element_type=...  5.91 us
    all_to_all x1, starting transfers between devices, per_device(): lax.all_to_all(send_data, 'sector', split_axis=0, concat_axis=0, tiled=True)  4.43 us
    reshape x1, local copies, waits for them, and re-layouts, cut_along(): return jnp.moveaxis(x.reshape(*before, devices, -1, *after), dim, 0)  3.19 us
  transfers between devices with their start and end apart: 3, of which 3 were waited for; matrix products, arithmetic and copies ran while one was open for 6% of the time, Pallas kernels for 0%

commit v1 on v0

v1 whole, which is shorter than its diff:
```python
import functools

import jax
import jax.numpy as jnp
from jax import lax
from jax.experimental import pallas as pl
from jax.experimental.pallas import tpu as pltpu
from jax.sharding import PartitionSpec as P

MESH = pl.DeviceIdType.MESH
F32, BF16, I32 = jnp.float32, jnp.bfloat16, jnp.int32
NB = 4
N = 512
RING = 4
SHARE = 32
W = 128
CHUNKS = 2
NS = 32
SLOT_ROWS = 16


def iota(shape, dim):
    return lax.broadcasted_iota(I32, shape, dim)


def one_hot_rows(chosen, base):
    lane = iota((NS, 128), 1)
    first = jnp.min(jnp.where(chosen, lane, 999), axis=1, keepdims=True)
    last = jnp.max(jnp.where(chosen, lane, -1), axis=1, keepdims=True)
    none = 256.0
    at_first = jnp.sum(jnp.where(lane == first, base, 0), axis=1, keepdims=True).astype(F32)
    at_last = jnp.sum(jnp.where(lane == last, base, 0), axis=1, keepdims=True).astype(F32)
    slot0 = jnp.where(first < 999, at_first, none)
    slot1 = jnp.where(last > first, at_last, none)
    both = jnp.where(lane < 64, slot0, slot1).astype(BF16)
    spread = (iota((NS * SLOT_ROWS, NS), 0) // SLOT_ROWS == iota((NS * SLOT_ROWS, NS), 1)).astype(F32).astype(BF16)
    rows = jnp.dot(spread, both, preferred_element_type=F32)
    inner = iota((NS * SLOT_ROWS, 1), 0) % SLOT_ROWS
    value = jnp.where(inner < 8, rows[:, 0:1], rows[:, 64:65]).astype(I32)
    value = jnp.where(value < 256, value + inner % 8, -1)
    return (iota((NS * SLOT_ROWS, 256), 1) == value).astype(F32).astype(BF16)


def kernel(
    wf_hbm, le_hbm, re_hbm, mask_hbm, size_hbm, owner_hbm, block_hbm,
    out_ref,
    wf, le, re, prod, r1, f1, q, r2, f2, pieces, sbuf, arr, tab, row, place, collect, outv,
    mask_s, size_s, owner_s, block_s,
    load_sem, small_sem, ss1, rs1, ss2, rs2, ssb, rsb, ssm, rsm, out_sem,
):
    m = lax.axis_index("mpo")
    s = lax.axis_index("sector")
    y, x = m // RING, m % RING

    loads = {}

    def load(key, src, dst, sem):
        c = pltpu.make_async_copy(src, dst, sem)
        c.start()
        loads[key] = c

    load("mask", mask_hbm, mask_s, small_sem.at[0])
    load("size", size_hbm, size_s, small_sem.at[1])
    load("owner", owner_hbm, owner_s, small_sem.at[2])
    load("block", block_hbm, block_s, small_sem.at[3])
    for b in range(NB):
        load(("wf", b), wf_hbm.at[b], wf.at[b], load_sem.at[b, 0])
        load(("re", b), re_hbm.at[0, b], re.at[b], load_sem.at[b, 1])
        load(("le", b), le_hbm.at[0, b], le.at[b], load_sem.at[b, 2])

    def ring_device(axis, delta):
        if axis == 0:
            return y * RING + (x + delta + RING) % RING
        return ((y + delta + RING) % RING) * RING + x

    def ring_pos(axis, delta):
        return ((x if axis == 0 else y) + delta + RING) % RING

    barrier = pltpu.get_barrier_semaphore()
    for axis in (0, 1):
        for delta in (1, -1):
            pl.semaphore_signal(barrier, inc=1, device_id={"mpo": ring_device(axis, delta), "sector": s}, device_id_type=MESH)

    @pl.loop(1, NS)
    def _(d):
        pl.semaphore_signal(barrier, inc=1, device_id={"mpo": m, "sector": (s + d) % NS}, device_id_type=MESH)

    for key in ("mask", "size", "owner", "block"):
        loads[key].wait()

    started = []

    def send(src, dst, ss, rs, dev):
        c = pltpu.make_async_remote_copy(
            src_ref=src, dst_ref=dst, send_sem=ss, recv_sem=rs, device_id={"mpo": dev, "sector": s}, device_id_type=MESH
        )
        c.start()
        started.append(c)

    def wait_recv(dst, ss, rs):
        pltpu.make_async_remote_copy(
            src_ref=dst, dst_ref=dst, send_sem=ss, recv_sem=rs, device_id={"mpo": m, "sector": s}, device_id_type=MESH
        ).wait_recv()

    def compute(j, b):
        if j == 0:
            loads[("wf", b)].wait()
            size = size_s[b] * mask_s[0, b]
            live = (iota((N, N), 0) < size) & (iota((N, N), 1) < size)
            wf[b] = jnp.where(live, wf[b], jnp.zeros((), BF16))
            loads[("re", b)].wait()
        rhs = jnp.concatenate([re[b, j * W : (j + 1) * W], re[b, 256 + j * W : 256 + (j + 1) * W]], axis=0)
        right = lax.dot_general(wf[b], rhs, (((1,), (1,)), ((), ())), preferred_element_type=F32).astype(BF16)
        if j == 0:
            loads[("le", b)].wait()
        out = jnp.dot(le[b], right, preferred_element_type=F32).astype(BF16)
        prod[j, 0, b] = out[:, :W].reshape(RING, RING, SHARE, W)
        prod[j, 1, b] = out[:, W:].reshape(RING, RING, SHARE, W)

    def part(g, j, b, pos):
        return prod.at[j, 0, b, :, pos] if g == 0 else prod.at[j, 1, b, pos]

    def step1(j, b):
        d = 1 if b < 2 else -1
        for g in (0, 1):
            send(part(g, j, b, ring_pos(g, 2 * d)), r1.at[j, g, b, 0], ss1.at[j, g, b, 0], rs1.at[j, g, b, 0], ring_device(g, d))
            send(part(g, j, b, ring_pos(g, -d)), r1.at[j, g, b, 2], ss1.at[j, g, b, 2], rs1.at[j, g, b, 2], ring_device(g, -d))

    def step2(j, b):
        d = 1 if b < 2 else -1
        for g in (0, 1):
            wait_recv(r1.at[j, g, b, 0], ss1.at[j, g, b, 0], rs1.at[j, g, b, 0])
            own = part(g, j, b, ring_pos(g, d))[...]
            f1[j, g, b] = (own.astype(F32) + r1[j, g, b, 0].astype(F32)).astype(BF16)
            send(f1.at[j, g, b], r1.at[j, g, b, 1], ss1.at[j, g, b, 1], rs1.at[j, g, b, 1], ring_device(g, d))

    def final1(j, b):
        for g in (0, 1):
            for t in (1, 2):
                wait_recv(r1.at[j, g, b, t], ss1.at[j, g, b, t], rs1.at[j, g, b, t])
            own = part(g, j, b, ring_pos(g, 0))[...]
            q[j, g, b] = (own.astype(F32) + r1[j, g, b, 1].astype(F32) + r1[j, g, b, 2].astype(F32)).astype(BF16)

    def part2(g, j, h, pos):
        return q.at[j, g, pl.ds(2 * h, 2), pos]

    def step3(j, h):
        d = 1 if h == 0 else -1
        for g in (0, 1):
            a = 1 - g
            send(part2(g, j, h, ring_pos(a, 2 * d)), r2.at[j, g, h, 0], ss2.at[j, g, h, 0], rs2.at[j, g, h, 0], ring_device(a, d))
            send(part2(g, j, h, ring_pos(a, -d)), r2.at[j, g, h, 2], ss2.at[j, g, h, 2], rs2.at[j, g, h, 2], ring_device(a, -d))

    def step4(j, h):
        d = 1 if h == 0 else -1
        for g in (0, 1):
            a = 1 - g
            wait_recv(r2.at[j, g, h, 0], ss2.at[j, g, h, 0], rs2.at[j, g, h, 0])
            own = part2(g, j, h, ring_pos(a, d))[...]
            f2[j, g, h] = (own.astype(F32) + r2[j, g, h, 0].astype(F32)).astype(BF16)
            send(f2.at[j, g, h], r2.at[j, g, h, 1], ss2.at[j, g, h, 1], rs2.at[j, g, h, 1], ring_device(a, d))

    def final2(j):
        for h in (0, 1):
            for g in (0, 1):
                a = 1 - g
                for t in (1, 2):
                    wait_recv(r2.at[j, g, h, t], ss2.at[j, g, h, t], rs2.at[j, g, h, t])
                own = part2(g, j, h, ring_pos(a, 0))[...]
                total = own.astype(F32) + r2[j, g, h, 1].astype(F32) + r2[j, g, h, 2].astype(F32)
                for i in (0, 1):
                    b = 2 * h + i
                    size = size_s[b]
                    live = (m * SHARE + iota((SHARE, W), 0) < size) & (g * 256 + j * W + iota((SHARE, W), 1) < size)
                    pieces[j, g * NB + b] = jnp.where(live, total[i], 0.0).astype(BF16)
        packed = jnp.dot(place[...], pieces[j].reshape(256, W), preferred_element_type=F32).astype(BF16)
        sbuf[j] = packed.reshape(NS, SLOT_ROWS, W)
        own_copy = pltpu.make_async_copy(sbuf.at[j, s], arr.at[j, s], rsb.at[j])
        own_copy.start()

        @pl.loop(1, NS)
        def _(i):
            peer = (s + peer_offset(i)) % NS
            pltpu.make_async_remote_copy(
                src_ref=sbuf.at[j, peer], dst_ref=arr.at[j, s], send_sem=ssb.at[j], recv_sem=rsb.at[j],
                device_id={"mpo": m, "sector": peer}, device_id_type=MESH,
            ).start()

    def peer_offset(i):
        return NS // 2 + (1 - 2 * (i % 2)) * (i // 2) + 0 * i

    def collect_chunk(j):
        pltpu.make_async_copy(arr.at[j], arr.at[j], rsb.at[j]).wait()
        got = arr[j].reshape(NS * SLOT_ROWS, W)
        res = lax.dot_general(collect[...], got, (((0,), (0,)), ((), ())), preferred_element_type=F32).astype(BF16)
        for c in (0, 1):
            outv[:, :, c * 256 + j * W : c * 256 + (j + 1) * W] = res[c * 128 : (c + 1) * 128].reshape(NB, SHARE, W)

    def make_row():
        lane = iota((1, 128), 1)
        acc = jnp.full((1, 128), 4 * NS, I32)
        for b in range(NB):
            for k in range(8):
                acc = jnp.where(lane == b * 8 + k, owner_s[0, b, k] * 4 + block_s[0, b, k], acc)
        row[...] = acc

    def send_rows():
        pltpu.make_async_copy(row, tab.at[s], rsm).start()

        @pl.loop(1, NS)
        def _(i):
            peer = (s + peer_offset(i)) % NS
            pltpu.make_async_remote_copy(
                src_ref=row, dst_ref=tab.at[s], send_sem=ssm, recv_sem=rsm,
                device_id={"mpo": m, "sector": peer}, device_id_type=MESH,
            ).start()

    lane_p = iota((NS, 128), 1)
    base_of = (lane_p % 2) * 128 + ((lane_p // 2) % 4) * 8

    def make_place():
        table = jnp.broadcast_to(row[...], (NS, 128))
        chosen = table // 4 == iota((NS, 128), 0)
        place[...] = one_hot_rows(chosen, base_of + (lane_p // 8) * 32)

    def make_collect():
        pltpu.make_async_copy(tab, tab, rsm).wait()
        table = tab[...].reshape(NS, 128)
        chosen = table // 4 == s
        collect[...] = one_hot_rows(chosen, base_of + (table % 4) * 32)

    make_row()
    compute(0, 0)
    pl.semaphore_wait(barrier, 4 + NS - 1)
    step1(0, 0)
    send_rows()
    for b in range(1, NB):
        compute(0, b)
        step1(0, b)
    make_place()
    compute(1, 0)
    step1(1, 0)
    step2(0, 0)
    compute(1, 1)
    step1(1, 1)
    step2(0, 1)
    compute(1, 2)
    step1(1, 2)
    step2(0, 2)
    final1(0, 0)
    final1(0, 1)
    step3(0, 0)
    compute(1, 3)
    step1(1, 3)
    step2(0, 3)
    final1(0, 2)
    final1(0, 3)
    step3(0, 1)
    step2(1, 0)
    make_collect()
    step4(0, 0)
    step2(1, 1)
    step4(0, 1)
    step2(1, 2)
    final2(0)
    step2(1, 3)
    final1(1, 0)
    final1(1, 1)
    step3(1, 0)
    final1(1, 2)
    final1(1, 3)
    step3(1, 1)
    step4(1, 0)
    step4(1, 1)
    final2(1)
    collect_chunk(0)
    collect_chunk(1)
    copy_out = pltpu.make_async_copy(outv, out_ref, out_sem)
    copy_out.start()
    for c in started:
        c.wait_send()
    for j in range(CHUNKS):
        pltpu.make_async_copy(arr.at[j, pl.ds(0, NS - 1)], arr.at[j, pl.ds(0, NS - 1)], ssb.at[j]).wait()
    pltpu.make_async_copy(tab.at[pl.ds(0, NS - 1)], tab.at[pl.ds(0, NS - 1)], ssm).wait()
    copy_out.wait()


def per_device(wavefunction, left_env, right_env, mpo_mask, block_size, route_owner, route_block):
    anyspec = pl.BlockSpec(memory_space=pl.ANY)
    dma = pltpu.SemaphoreType.DMA
    return pl.pallas_call(
        kernel,
        out_shape=jax.ShapeDtypeStruct((NB, SHARE, N), BF16),
        in_specs=[anyspec] * 7,
        out_specs=anyspec,
        scratch_shapes=[
            pltpu.VMEM((NB, N, N), BF16),
            pltpu.VMEM((NB, N, N), BF16),
            pltpu.VMEM((NB, N, N), BF16),
            pltpu.VMEM((CHUNKS, 2, NB, RING, RING, SHARE, W), BF16),
            pltpu.VMEM((CHUNKS, 2, NB, 3, RING, SHARE, W), BF16),
            pltpu.VMEM((CHUNKS, 2, NB, RING, SHARE, W), BF16),
            pltpu.VMEM((CHUNKS, 2, NB, RING, SHARE, W), BF16),
            pltpu.VMEM((CHUNKS, 2, 2, 3, 2, SHARE, W), BF16),
            pltpu.VMEM((CHUNKS, 2, 2, 2, SHARE, W), BF16),
            pltpu.VMEM((CHUNKS, 2 * NB, SHARE, W), BF16),
            pltpu.VMEM((CHUNKS, NS, SLOT_ROWS, W), BF16),
            pltpu.VMEM((CHUNKS, NS, SLOT_ROWS, W), BF16),
            pltpu.VMEM((NS, 1, 128), I32),
            pltpu.VMEM((1, 128), I32),
            pltpu.VMEM((NS * SLOT_ROWS, 256), BF16),
            pltpu.VMEM((NS * SLOT_ROWS, 256), BF16),
            pltpu.VMEM((NB, SHARE, N), BF16),
            pltpu.SMEM((1, NB), I32),
            pltpu.SMEM((NB,), I32),
            pltpu.SMEM((1, NB, 8), I32),
            pltpu.SMEM((1, NB, 8), I32),
            dma((NB, 3)),
            dma((4,)),
            dma((CHUNKS, 2, NB, 3)),
            dma((CHUNKS, 2, NB, 3)),
            dma((CHUNKS, 2, 2, 3)),
            dma((CHUNKS, 2, 2, 3)),
            dma((CHUNKS,)),
            dma((CHUNKS,)),
            dma,
            dma,
            dma,
        ],
        compiler_params=pltpu.CompilerParams(collective_id=0, has_side_effects=True, vmem_limit_bytes=67043328),
    )(wavefunction, left_env, right_env, mpo_mask, block_size, route_owner, route_block)


def solution(mesh):
    placed = (
        P("sector", None, None),
        P("mpo", "sector", None, None),
        P("mpo", "sector", None, None),
        P("mpo", "sector"),
        P("sector"),
        P("mpo", "sector", None),
        P("mpo", "sector", None),
    )
    return jax.shard_map(per_device, mesh=mesh, in_specs=placed, out_specs=P("sector", "mpo", None), check_vma=False)
```

time: 106 us -> 58.8 us (0.55)
  Pallas kernels: 0 us -> 57.1 us
  waiting for transfers between devices: 51.8 us -> 0 us
  starting transfers between devices: 35.4 us -> 0 us
  matrix products: 6.42 us -> 0 us
  local copies, waits for them, and re-layouts: 6.6 us -> 1.57 us
  other arithmetic: 4.95 us -> 0 us
    pallas_call x0 -> x1, Pallas kernels: none -> 57.1 us  [per_device(): pl.pallas_call(kernel, out_shape=jax.ShapeDtypeStruct((NB, SHARE, N), BF1...]
    all_to_all x3 -> x0, waiting for transfers between devices: 51.8 us -> none  [the longest x1 23.2 us: sent_and_summed(): lax.all_to_all(tiles, axis, split_axis=0, concat_axis=0, tiled=True)]
    all_to_all x3 -> x0, starting transfers between devices: 35.4 us -> none  [the longest x1 23.2 us: per_device(): lax.all_to_all(send_code, 'sector', split_axis=0, concat_axis=0, tiled=True)]
    dot_general x3 -> x0, matrix products: 6.42 us -> none  [the longest x1 5.91 us: per_device(): jnp.einsum('bij,bjk->ibk', left_rows, right_part, preferred_element_type=...]
    reshape x3 -> x0, local copies, waits for them, and re-layouts: 4.17 us -> none  [the longest x1 3.19 us: cut_along(): return jnp.moveaxis(x.reshape(*before, devices, -1, *after), dim, 0)]
    reduce_sum x3 -> x0, other arithmetic: 2.18 us -> none  [the longest x1 1.91 us: sent_and_summed(): return arrived.astype(jnp.float32).sum(axis=0)]
  transfers between devices with their start and end apart: 3 -> 0, of which waited for: 3 -> 0; matrix products, arithmetic and copies ran while one was open for 6% -> 0% of each run, Pallas kernels for 0% -> 0%
where the time goes in v1:
time: 58.8 us; the launch traced here: 58.7 us
  Pallas kernels  57.1 us (97%)
  local copies, waits for them, and re-layouts  1.57 us (3%)
    pallas_call x1, Pallas kernels, per_device(): pl.pallas_call(kernel, out_shape=jax.ShapeDtypeStruct((NB, SHARE, N), BF1...  57.1 us
    unnamed x1, local copies, waits for them, and re-layouts  1.57 us

profile of v1, /device:TPU:1, one launch (start us, length us, event | category | flops | bytes accessed | tf_op | source)
XLA Modules:
  0.0 58.7 jit_solution(11686657834040916495)
XLA Ops:
  0.0 57.1 %shard_map.73 = bf16[4,32,512]{2,1,0:T(8,128)(2,1)} custom-call(bf16[4,512,512]{2,1,0:T(8,128)(2,1)} %wf_hbm.1, bf16[1,4,512,512]{3,2,1,0:T(8,128)(2,1)} %le_hbm.1, bf16[1,4,512,512]{3,2,1,0:T(8,128)(2,1)} %re_hbm.1, s32[1,4]{1,0:T(1,128)} %mask_hbm.1, s32[4]{0:T(128)} %size_hbm.1, s32[1,4,8]{2,1,0:T(4,128)} %owner_hbm.1, s32[1,4,8]{2,1,0:T(4,128)} %block_hbm.1), custom_call_target="tpu_custom_call" | custom-call | tf_op jit(solution)/shard_map/pallas_call | solution.py:291
  57.1 1.6 %copy.9 = bf16[4,32,512]{2,1,0:T(8,128)(2,1)} copy(bf16[4,32,512]{2,1,0:T(8,128)(2,1)} %shard_map.73) | data formatting | bytes 262144

commit v2 on v0

v2 whole, which is shorter than its diff:
```python
import jax
import jax.numpy as jnp
from jax import lax
from jax.experimental import pallas as pl
from jax.experimental.pallas import tpu as pltpu
from jax.sharding import PartitionSpec as P

MESH = pl.DeviceIdType.MESH
F32, BF16, I32 = jnp.float32, jnp.bfloat16, jnp.int32
NB = 4
N = 512
RING = 4
SHARE = 32
CHUNKS = 4
CW = 64
W = 128
NS = 32
PR = 8

GROUPS = ((0, (0,)), (0, (2,)), (0, (1, 3)), (1, (0, 2)), (1, (1, 3)))
ORDER = (
    ("C", 0, 0), ("S1", 0, 0), ("C", 1, 0), ("S1", 1, 2), ("P", 0, 0), ("S1", 0, 2), ("S1", 1, 0), ("Z", 1, 0),
    ("C", 2, 0), ("S1", 0, 1), ("S1", 0, 3), ("S1", 1, 3), ("S1", 1, 1), ("Z", 2, 0), ("C", 3, 0), ("F1", 0, 0),
    ("F1", 1, 2), ("S1", 2, 0), ("Z", 3, 0), ("S1", 2, 2), ("C", 4, 0), ("F1", 0, 2), ("F1", 0, 1), ("F1", 0, 3),
    ("S1", 2, 1), ("S1", 2, 3), ("F1", 1, 0), ("Z", 4, 0), ("F1", 1, 1), ("F1", 1, 3), ("Z", 5, 0), ("S1", 3, 1),
    ("F2", 0, 0), ("F2", 1, 2), ("S1", 3, 2), ("S1", 3, 0), ("S1", 3, 3), ("F1", 2, 0), ("F2", 0, 2), ("F1", 2, 2),
    ("F2", 0, 3), ("F2", 0, 1), ("B", 0, 0), ("F1", 2, 1), ("F1", 2, 3), ("F2", 1, 3), ("F2", 1, 0), ("F2", 1, 1),
    ("B", 1, 0), ("F1", 3, 1), ("F1", 3, 2), ("F1", 3, 0), ("F1", 3, 3), ("F2", 2, 3), ("F2", 2, 2), ("F2", 2, 0),
    ("F2", 2, 1), ("B", 2, 0), ("F2", 3, 1), ("F2", 3, 2), ("F2", 3, 0), ("F2", 3, 3), ("B", 3, 0), ("Q", 0, 0),
    ("K", 0, 0), ("K", 1, 0), ("K", 2, 0), ("K", 3, 0),
)


def iota(shape, dim):
    return lax.broadcasted_iota(I32, shape, dim)


def one_hot_rows(chosen, base):
    lane = iota((NS, 128), 1)
    first = jnp.min(jnp.where(chosen, lane, 999), axis=1, keepdims=True)
    last = jnp.max(jnp.where(chosen, lane, -1), axis=1, keepdims=True)
    at_first = jnp.sum(jnp.where(lane == first, base, 0), axis=1, keepdims=True).astype(F32)
    at_last = jnp.sum(jnp.where(lane == last, base, 0), axis=1, keepdims=True).astype(F32)
    slot0 = jnp.where(first < 999, at_first, 256.0)
    slot1 = jnp.where(last > first, at_last, 256.0)
    both = jnp.where(lane < 64, slot0, slot1).astype(BF16)
    spread = (iota((NS * PR, NS), 0) // PR == iota((NS * PR, NS), 1)).astype(F32).astype(BF16)
    rows = jnp.dot(spread, both, preferred_element_type=F32)
    inner = iota((NS * PR, 1), 0) % PR
    out = []
    for at in (0, 64):
        value = rows[:, at : at + 1].astype(I32)
        value = jnp.where(value < 256, value + inner, -1)
        out.append((iota((NS * PR, 256), 1) == value).astype(F32))
    return out


def kernel(
    wf_hbm, le_hbm, re_hbm, mask_hbm, size_hbm, owner_hbm, block_hbm,
    out_ref,
    wf, le, re, prod, r1, q, r2, pieces, sbuf, arr, tab, row, place, collect, half,
    mask_s, size_s, owner_s, block_s,
    load_sem, small_sem, ss1, rs1, ss2, rs2, ssb, rsb, ssm, rsm, news,
):
    m = lax.axis_index("mpo")
    s = lax.axis_index("sector")
    y, x = m // RING, m % RING
    loads = {}

    def load(key, src, dst, sem):
        c = pltpu.make_async_copy(src, dst, sem)
        c.start()
        loads[key] = c

    def ring_device(axis, delta):
        if axis == 0:
            return y * RING + (x + delta + RING) % RING
        return ((y + delta + RING) % RING) * RING + x

    def ring_pos(axis, delta):
        return ((x if axis == 0 else y) + delta + RING) % RING

    def tell(sem, dev, sector):
        pl.semaphore_signal(sem, inc=1, device_id={"mpo": dev, "sector": sector}, device_id_type=MESH)

    partner = s + 1 - 2 * (s % 2)
    barrier = pltpu.get_barrier_semaphore()
    for axis in (0, 1):
        for delta in (1, -1, 2):
            tell(barrier, ring_device(axis, delta), s)
    tell(barrier, m, (s + 2) % NS)
    tell(barrier, m, (s + NS - 2) % NS)
    tell(barrier, m, partner)

    load("mask", mask_hbm, mask_s, small_sem.at[0])
    load("size", size_hbm, size_s, small_sem.at[1])
    for b in (0, 2, 1, 3):
        load(("wf", b), wf_hbm.at[b], wf.at[b], load_sem.at[b, 0])
        load(("re", b, 0), re_hbm.at[0, b, pl.ds(0, W)], re.at[b, pl.ds(0, W)], load_sem.at[b, 1])
        load(("re", b, 1), re_hbm.at[0, b, pl.ds(256, W)], re.at[b, pl.ds(256, W)], load_sem.at[b, 2])
        load(("le", b), le_hbm.at[0, b], le.at[b], load_sem.at[b, 3])
    load("owner", owner_hbm, owner_s, small_sem.at[2])
    load("block", block_hbm, block_s, small_sem.at[3])
    for b in (0, 2, 1, 3):
        load(("re", b, 2), re_hbm.at[0, b, pl.ds(W, W)], re.at[b, pl.ds(W, W)], load_sem.at[b, 4])
        load(("re", b, 3), re_hbm.at[0, b, pl.ds(256 + W, W)], re.at[b, pl.ds(256 + W, W)], load_sem.at[b, 5])
    loads["mask"].wait()
    loads["size"].wait()

    started = []

    def send(src, dst, ss, rs, dev):
        c = pltpu.make_async_remote_copy(
            src_ref=src, dst_ref=dst, send_sem=ss, recv_sem=rs, device_id={"mpo": dev, "sector": s}, device_id_type=MESH
        )
        c.start()
        started.append(c)

    def arrived(dst, ss, rs):
        pltpu.make_async_remote_copy(
            src_ref=dst, dst_ref=dst, send_sem=ss, recv_sem=rs, device_id={"mpo": m, "sector": s}, device_id_type=MESH
        ).wait_recv()

    entered = [False]

    def compute(group):
        jp, blocks = GROUPS[group]
        rights = []
        for b in blocks:
            size = size_s[b] * mask_s[0, b]
            if jp == 0:
                loads[("wf", b)].wait()
                live = (iota((1, N), 1) < size).astype(F32).astype(BF16)
                wf[b] = wf[b] * live
            loads[("re", b, 2 * jp)].wait()
            loads[("re", b, 2 * jp + 1)].wait()
            if jp == 0:
                loads[("le", b)].wait()
        for b in blocks:
            size = size_s[b] * mask_s[0, b]
            rhs = jnp.concatenate(
                [re[b, c * 256 + (2 * jp + h) * CW : c * 256 + (2 * jp + h + 1) * CW] for h in (0, 1) for c in (0, 1)],
                axis=0,
            )
            right = lax.dot_general(wf[b], rhs, (((1,), (1,)), ((), ())), preferred_element_type=F32)
            rights.append(jnp.where(iota((N, 1), 0) < size, right, 0.0).astype(BF16))
        for b, right in zip(blocks, rights):
            out = jnp.dot(le[b], right, preferred_element_type=F32).astype(BF16)
            for h in (0, 1):
                prod[2 * jp + h, b] = out[:, h * W : (h + 1) * W].reshape(RING, RING, SHARE, W)

    def axis_of(b):
        return 0 if b < 2 else 1

    def part(j, b, pos):
        return prod.at[j, b, :, pos] if axis_of(b) == 0 else prod.at[j, b, pos]

    def step1(j, b):
        if not entered[0]:
            entered[0] = True
            pl.semaphore_wait(barrier, 9)
        a = axis_of(b)
        for t, d in ((0, 2), (1, 1), (2, -1)):
            send(part(j, b, ring_pos(a, d)), r1.at[j, b, t], ss1.at[j, b, t], rs1.at[j, b, t], ring_device(a, d))

    def final1(j, b):
        a = axis_of(b)
        for t in (1, 2, 0):
            arrived(r1.at[j, b, t], ss1.at[j, b, t], rs1.at[j, b, t])
        total = part(j, b, ring_pos(a, 0))[...].astype(F32)
        for t in (0, 1, 2):
            total = total + r1[j, b, t].astype(F32)
        q[j, b] = total.astype(BF16)
        a = 1 - a
        for t, d in ((0, 2), (1, 1), (2, -1)):
            send(q.at[j, b, ring_pos(a, d)], r2.at[j, b, t], ss2.at[j, b, t], rs2.at[j, b, t], ring_device(a, d))

    def final2(j, b):
        a = 1 - axis_of(b)
        for t in (1, 2, 0):
            arrived(r2.at[j, b, t], ss2.at[j, b, t], rs2.at[j, b, t])
        total = q[j, b, ring_pos(a, 0)].astype(F32)
        for t in (0, 1, 2):
            total = total + r2[j, b, t].astype(F32)
        lane = iota((SHARE, W), 1)
        column = (lane // CW) * 256 + j * CW + lane % CW
        live = (m * SHARE + iota((SHARE, W), 0) < size_s[b]) & (column < size_s[b])
        pieces[j, b] = jnp.where(live, total, 0.0)

    def peer_at(i):
        return (s + NS // 2 + (1 - 2 * (i % 2)) * (i // 2)) % NS

    def to_peers(src_of, dst, ss, rs):
        @pl.loop(1, NS)
        def _(i):
            peer = peer_at(i)
            pltpu.make_async_remote_copy(
                src_ref=src_of(peer), dst_ref=dst, send_sem=ss, recv_sem=rs,
                device_id={"mpo": m, "sector": peer}, device_id_type=MESH,
            ).start()

    low = iota((NB * SHARE, W), 1) < CW

    def exchange(j):
        share = pieces[j].reshape(NB * SHARE, W)
        turned = pltpu.roll(share, CW, 1)
        rhs = jnp.concatenate([jnp.where(low, share, turned), jnp.where(low, turned, share)], axis=0).astype(BF16)
        slot0 = jnp.dot(place[0], rhs, preferred_element_type=F32)
        slot1 = jnp.dot(place[1], rhs, preferred_element_type=F32)
        packed = jnp.where(iota((NS * PR, W), 1) < CW, slot0, slot1).astype(BF16)
        sbuf[j] = packed.reshape(NS, PR, W)
        pltpu.make_async_copy(sbuf.at[j, s], arr.at[j, s], rsb.at[j]).start()
        to_peers(lambda peer: sbuf.at[j, peer], arr.at[j, s], ssb.at[j], rsb.at[j])

    def collect_chunk(j):
        pltpu.make_async_copy(arr.at[j], arr.at[j], rsb.at[j]).wait()
        got = arr[j].reshape(NS * PR, W)
        slot0 = jnp.dot(collect[0], got, preferred_element_type=F32)
        slot1 = jnp.dot(collect[1], got, preferred_element_type=F32)
        if j % 2 == 0:
            half[...] = slot0 + pltpu.roll(slot1, CW, 1)
        else:
            both = jnp.where(iota((NS * PR, W), 1) < CW, half[...], slot1 + pltpu.roll(slot0, CW, 1)).astype(BF16)
            for c in (0, 1):
                at = c * 256 + (j // 2) * W
                out_ref[:, :, at : at + W] = both[c * 128 : (c + 1) * 128].reshape(NB, SHARE, W)

    lane_p = iota((NS, 128), 1)
    base_of = (lane_p % 2) * 128 + ((lane_p // 2) % 4) * PR

    def make_place():
        loads["owner"].wait()
        loads["block"].wait()
        lane = iota((1, 128), 1)
        acc = jnp.full((1, 128), 4 * NS, I32)
        for b in range(NB):
            for k in range(8):
                acc = jnp.where(lane == b * 8 + k, owner_s[0, b, k] * 4 + block_s[0, b, k], acc)
        row[...] = acc
        table = jnp.broadcast_to(acc, (NS, 128))
        chosen = table // 4 == iota((NS, 128), 0)
        for t, one_hot in enumerate(one_hot_rows(chosen, base_of + (lane_p // 8) * SHARE)):
            place[t] = one_hot.astype(BF16)

    def make_collect():
        pltpu.make_async_copy(tab, tab, rsm).wait()
        table = tab[...].reshape(NS, 128)
        chosen = table // 4 == s
        for t, one_hot in enumerate(one_hot_rows(chosen, base_of + (table % 4) * SHARE)):
            collect[t] = one_hot.T.astype(BF16)

    def sector_news(i):
        if i <= 3:
            if i >= 2:
                pl.semaphore_wait(news.at[i - 2], 2)
            step = 2 ** i
            tell(news.at[i - 1], m, (s + step) % NS)
            tell(news.at[i - 1], m, (s + NS - step) % NS)
        elif i == 4:
            pl.semaphore_wait(news.at[2], 2)
            tell(news.at[3], m, partner)
        else:
            pl.semaphore_wait(news.at[3], 1)
            pltpu.make_async_copy(row, tab.at[s], rsm).start()
            to_peers(lambda peer: row, tab.at[s], ssm, rsm)

    for name, j, b in ORDER:
        if name == "C":
            compute(j)
        elif name == "S1":
            step1(j, b)
        elif name == "F1":
            final1(j, b)
        elif name == "F2":
            final2(j, b)
        elif name == "B":
            exchange(j)
        elif name == "K":
            collect_chunk(j)
        elif name == "P":
            make_place()
        elif name == "Q":
            make_collect()
        else:
            sector_news(j)
    for c in started:
        c.wait_send()
    for j in range(CHUNKS):
        pltpu.make_async_copy(arr.at[j, pl.ds(0, NS - 1)], arr.at[j, pl.ds(0, NS - 1)], ssb.at[j]).wait()
    pltpu.make_async_copy(tab.at[pl.ds(0, NS - 1)], tab.at[pl.ds(0, NS - 1)], ssm).wait()


def per_device(wavefunction, left_env, right_env, mpo_mask, block_size, route_owner, route_block):
    in_hbm = pl.BlockSpec(memory_space=pltpu.HBM)
    dma = pltpu.SemaphoreType.DMA
    vmem = pltpu.VMEM
    return pl.pallas_call(
        kernel,
        out_shape=jax.ShapeDtypeStruct((NB, SHARE, N), BF16),
        in_specs=[in_hbm] * 7,
        out_specs=pl.BlockSpec(memory_space=pltpu.VMEM),
        scratch_shapes=[
            vmem((NB, N, N), BF16),
            vmem((NB, N, N), BF16),
            vmem((NB, N, N), BF16),
            vmem((CHUNKS, NB, RING, RING, SHARE, W), BF16),
            vmem((CHUNKS, NB, 3, RING, SHARE, W), BF16),
            vmem((CHUNKS, NB, RING, SHARE, W), BF16),
            vmem((CHUNKS, NB, 3, SHARE, W), BF16),
            vmem((CHUNKS, NB, SHARE, W), F32),
            vmem((CHUNKS, NS, PR, W), BF16),
            vmem((CHUNKS, NS, PR, W), BF16),
            vmem((NS, 1, 128), I32),
            vmem((1, 128), I32),
            vmem((2, NS * PR, 256), BF16),
            vmem((2, 256, NS * PR), BF16),
            vmem((256, W), F32),
            pltpu.SMEM((1, NB), I32),
            pltpu.SMEM((NB,), I32),
            pltpu.SMEM((1, NB, 8), I32),
            pltpu.SMEM((1, NB, 8), I32),
            dma((NB, 6)),
            dma((4,)),
            dma((CHUNKS, NB, 3)),
            dma((CHUNKS, NB, 3)),
            dma((CHUNKS, NB, 3)),
            dma((CHUNKS, NB, 3)),
            dma((CHUNKS,)),
            dma((CHUNKS,)),
            dma,
            dma,
            pltpu.SemaphoreType.REGULAR((4,)),
        ],
        compiler_params=pltpu.CompilerParams(collective_id=0, has_side_effects=True, vmem_limit_bytes=67043328),
    )(wavefunction, left_env, right_env, mpo_mask, block_size, route_owner, route_block)


def solution(mesh):
    placed = (
        P("sector", None, None),
        P("mpo", "sector", None, None),
        P("mpo", "sector", None, None),
        P("mpo", "sector"),
        P("sector"),
        P("mpo", "sector", None),
        P("mpo", "sector", None),
    )
    return jax.shard_map(per_device, mesh=mesh, in_specs=placed, out_specs=P("sector", "mpo", None), check_vma=False)
```

time: 106 us -> 46.9 us (0.44)
  waiting for transfers between devices: 51.8 us -> 0 us
  Pallas kernels: 0 us -> 45.2 us
  starting transfers between devices: 35.4 us -> 0 us
  matrix products: 6.42 us -> 0 us
  local copies, waits for them, and re-layouts: 6.6 us -> 1.57 us
  other arithmetic: 4.95 us -> 0 us
    all_to_all x3 -> x0, waiting for transfers between devices: 51.8 us -> none  [the longest x1 23.2 us: sent_and_summed(): lax.all_to_all(tiles, axis, split_axis=0, concat_axis=0, tiled=True)]
    pallas_call x0 -> x1, Pallas kernels: none -> 45.2 us  [per_device(): pl.pallas_call(kernel, out_shape=jax.ShapeDtypeStruct((NB, SHARE, N), BF1...]
    all_to_all x3 -> x0, starting transfers between devices: 35.4 us -> none  [the longest x1 23.2 us: per_device(): lax.all_to_all(send_code, 'sector', split_axis=0, concat_axis=0, tiled=True)]
    dot_general x3 -> x0, matrix products: 6.42 us -> none  [the longest x1 5.91 us: per_device(): jnp.einsum('bij,bjk->ibk', left_rows, right_part, preferred_element_type=...]
    reshape x3 -> x0, local copies, waits for them, and re-layouts: 4.17 us -> none  [the longest x1 3.19 us: cut_along(): return jnp.moveaxis(x.reshape(*before, devices, -1, *after), dim, 0)]
    reduce_sum x3 -> x0, other arithmetic: 2.18 us -> none  [the longest x1 1.91 us: sent_and_summed(): return arrived.astype(jnp.float32).sum(axis=0)]
  transfers between devices with their start and end apart: 3 -> 0, of which waited for: 3 -> 0; matrix products, arithmetic and copies ran while one was open for 6% -> 0% of each run, Pallas kernels for 0% -> 0%
where the time goes in v2:
time: 46.9 us; the launch traced here: 46.8 us
  Pallas kernels  45.2 us (96%)
  local copies, waits for them, and re-layouts  1.57 us (3%)
    pallas_call x1, Pallas kernels, per_device(): pl.pallas_call(kernel, out_shape=jax.ShapeDtypeStruct((NB, SHARE, N), BF1...  45.2 us
    unnamed x1, local copies, waits for them, and re-layouts  1.57 us

profile of v2, /device:TPU:1, one launch (start us, length us, event | category | flops | bytes accessed | tf_op | source)
XLA Modules:
  0.0 46.8 jit_solution(16299134703979006755)
XLA Ops:
  0.0 45.2 %shard_map.73 = bf16[4,32,512]{2,1,0:T(8,128)(2,1)} custom-call(bf16[4,512,512]{2,1,0:T(8,128)(2,1)} %wf_hbm.1, bf16[1,4,512,512]{3,2,1,0:T(8,128)(2,1)} %le_hbm.1, bf16[1,4,512,512]{3,2,1,0:T(8,128)(2,1)} %re_hbm.1, s32[1,4]{1,0:T(1,128)} %mask_hbm.1, s32[4]{0:T(128)} %size_hbm.1, s32[1,4,8]{2,1,0:T(4,128)} %owner_hbm.1, s32[1,4,8]{2,1,0:T(4,128)} %block_hbm.1), custom_call_target="tpu_custom_call" | custom-call | tf_op jit(solution)/shard_map/pallas_call | solution.py:297
  45.2 1.6 %copy.9 = bf16[4,32,512]{2,1,0:T(8,128)(2,1)} copy(bf16[4,32,512]{2,1,0:T(8,128)(2,1)} %shard_map.73) | data formatting | bytes 262144

commit v3 on v2

--- a/solution.py
+++ b/solution.py
@@ -64,7 +64,7 @@
 ):
     m = lax.axis_index("mpo")
     s = lax.axis_index("sector")
-    y, x = m // RING, m % RING
+    y, x = lax.div(m, RING), lax.rem(m, RING)
     loads = {}
 
     def load(key, src, dst, sem):
@@ -74,27 +74,19 @@
 
     def ring_device(axis, delta):
         if axis == 0:
-            return y * RING + (x + delta + RING) % RING
-        return ((y + delta + RING) % RING) * RING + x
+            return y * RING + lax.rem(x + delta + RING, RING)
+        return lax.rem(y + delta + RING, RING) * RING + x
 
     def ring_pos(axis, delta):
-        return ((x if axis == 0 else y) + delta + RING) % RING
+        return lax.rem((x if axis == 0 else y) + delta + RING, RING)
 
     def tell(sem, dev, sector):
         pl.semaphore_signal(sem, inc=1, device_id={"mpo": dev, "sector": sector}, device_id_type=MESH)
 
-    partner = s + 1 - 2 * (s % 2)
-    barrier = pltpu.get_barrier_semaphore()
-    for axis in (0, 1):
-        for delta in (1, -1, 2):
-            tell(barrier, ring_device(axis, delta), s)
-    tell(barrier, m, (s + 2) % NS)
-    tell(barrier, m, (s + NS - 2) % NS)
-    tell(barrier, m, partner)
-
-    load("mask", mask_hbm, mask_s, small_sem.at[0])
-    load("size", size_hbm, size_s, small_sem.at[1])
     for b in (0, 2, 1, 3):
+        if b == 2:
+            load("mask", mask_hbm, mask_s, small_sem.at[0])
+            load("size", size_hbm, size_s, small_sem.at[1])
         load(("wf", b), wf_hbm.at[b], wf.at[b], load_sem.at[b, 0])
         load(("re", b, 0), re_hbm.at[0, b, pl.ds(0, W)], re.at[b, pl.ds(0, W)], load_sem.at[b, 1])
         load(("re", b, 1), re_hbm.at[0, b, pl.ds(256, W)], re.at[b, pl.ds(256, W)], load_sem.at[b, 2])
@@ -104,6 +96,15 @@
     for b in (0, 2, 1, 3):
         load(("re", b, 2), re_hbm.at[0, b, pl.ds(W, W)], re.at[b, pl.ds(W, W)], load_sem.at[b, 4])
         load(("re", b, 3), re_hbm.at[0, b, pl.ds(256 + W, W)], re.at[b, pl.ds(256 + W, W)], load_sem.at[b, 5])
+    partner = s + 1 - 2 * lax.rem(s, 2)
+    barrier = pltpu.get_barrier_semaphore()
+    for axis in (0, 1):
+        for delta in (1, -1, 2):
+            tell(barrier, ring_device(axis, delta), s)
+    tell(barrier, m, lax.rem(s + 2, NS))
+    tell(barrier, m, lax.rem(s + NS - 2, NS))
+    tell(barrier, m, partner)
+
     loads["mask"].wait()
     loads["size"].wait()
 
@@ -187,13 +188,9 @@
         live = (m * SHARE + iota((SHARE, W), 0) < size_s[b]) & (column < size_s[b])
         pieces[j, b] = jnp.where(live, total, 0.0)
 
-    def peer_at(i):
-        return (s + NS // 2 + (1 - 2 * (i % 2)) * (i // 2)) % NS
-
     def to_peers(src_of, dst, ss, rs):
-        @pl.loop(1, NS)
-        def _(i):
-            peer = peer_at(i)
+        for i in range(1, NS):
+            peer = lax.rem(s + (NS // 2 + (i // 2 if i % 2 else -(i // 2))), NS)
             pltpu.make_async_remote_copy(
                 src_ref=src_of(peer), dst_ref=dst, send_sem=ss, recv_sem=rs,
                 device_id={"mpo": m, "sector": peer}, device_id_type=MESH,
@@ -254,8 +251,8 @@
             if i >= 2:
                 pl.semaphore_wait(news.at[i - 2], 2)
             step = 2 ** i
-            tell(news.at[i - 1], m, (s + step) % NS)
-            tell(news.at[i - 1], m, (s + NS - step) % NS)
+            tell(news.at[i - 1], m, lax.rem(s + step, NS))
+            tell(news.at[i - 1], m, lax.rem(s + NS - step, NS))
         elif i == 4:
             pl.semaphore_wait(news.at[2], 2)
             tell(news.at[3], m, partner)
@@ -294,6 +291,8 @@
     in_hbm = pl.BlockSpec(memory_space=pltpu.HBM)
     dma = pltpu.SemaphoreType.DMA
     vmem = pltpu.VMEM
+    args = (wavefunction, left_env, right_env, mpo_mask, block_size, route_owner, route_block)
+    held = [pltpu.with_memory_space_constraint(a, pltpu.HBM) for a in args]
     return pl.pallas_call(
         kernel,
         out_shape=jax.ShapeDtypeStruct((NB, SHARE, N), BF16),
@@ -331,8 +330,8 @@
             dma,
             pltpu.SemaphoreType.REGULAR((4,)),
         ],
-        compiler_params=pltpu.CompilerParams(collective_id=0, has_side_effects=True, vmem_limit_bytes=67043328),
-    )(wavefunction, left_env, right_env, mpo_mask, block_size, route_owner, route_block)
+        compiler_params=pltpu.CompilerParams(collective_id=0, has_side_effects=True, vmem_limit_bytes=48 << 20),
+    )(*held)
 
 
 def solution(mesh):

time: 46.9 us -> 45.3 us (0.966)
  local copies, waits for them, and re-layouts: 1.57 us -> 0.66 us
  Pallas kernels: 45.2 us -> 44.5 us
    unnamed x1, local copies, waits for them, and re-layouts: 1.57 us -> 0.66 us
    pallas_call x1, Pallas kernels: 45.2 us -> 44.5 us  [per_device(): pl.pallas_call(kernel, out_shape=jax.ShapeDtypeStruct((NB, SHARE, N), BF1...]
where the time goes in v3:
time: 45.3 us; the launch traced here: 45.2 us
  Pallas kernels  44.5 us (98%)
  local copies, waits for them, and re-layouts  0.66 us (1%)
    pallas_call x1, Pallas kernels, per_device(): pl.pallas_call(kernel, out_shape=jax.ShapeDtypeStruct((NB, SHARE, N), BF1...  44.5 us

profile of v3, /device:TPU:1, one launch (start us, length us, event | category | flops | bytes accessed | tf_op | source)
XLA Modules:
  0.0 45.2 jit_solution(5786097503271785263)
XLA Ops:
  0.0 44.5 %shard_map.73 = bf16[4,32,512]{2,1,0:T(8,128)(2,1)S(1)} custom-call(bf16[4,512,512]{2,1,0:T(8,128)(2,1)} %wf_hbm.1, bf16[1,4,512,512]{3,2,1,0:T(8,128)(2,1)} %le_hbm.1, bf16[1,4,512,512]{3,2,1,0:T(8,128)(2,1)} %re_hbm.1, s32[1,4]{1,0:T(1,128)} %mask_hbm.1, s32[4]{0:T(128)} %size_hbm.1, s32[1,4,8]{2,1,0:T(4,128)} %owner_hbm.1, s32[1,4,8]{2,1,0:T(4,128)} %block_hbm.1), custom_call_target="tpu_custom_call" | custom-call | tf_op jit(solution)/shard_map/pallas_call | solution.py:296
  44.5 0.7 %copy.9 = bf16[4,32,512]{2,1,0:T(8,128)(2,1)} copy(bf16[4,32,512]{2,1,0:T(8,128)(2,1)S(1)} %shard_map.73) | data formatting | bytes 262144
